TPU v7x, 256 devices: a whole 4x4x8 slice. The times are simulated.
256 devices in a mesh: gx: 64 (over x, z, core), af: 4 (over y).
Axes of the slice: x: 4, y: 4, z: 8, core: 2. Of those that a mesh axis runs over, the one named last changes fastest.
Arguments:
- scalar_field: float32 [128, 512, 512], P('gx', 'af'), may hold values from -256 to 256
- plane_sketch: float32 [128, 2, 256], P('gx'), may hold values from -0.5 to 0.5
- second_sketch: float32 [512, 256], P('af'), may hold values from -0.25 to 0.25
- third_sketch: float32 [512, 256], replicated, may hold values from -0.25 to 0.25
- mixing: float32 [2, 256, 128], replicated, may hold values from -0.375 to 0.375
- plane_targets: int32 [128, 2], replicated, may hold values from 0 to 7
- plane_signs: int32 [128, 2], replicated, may hold values from 0 to 1
Outputs:
- factor_second: float32 [512, 128], P(('af', 'gx'))
- factor_third: float32 [512, 128], P(('gx', 'af'))
- core_sketch: float32 [128, 128, 128], P('gx', 'af')
Inputs may be any that keep to these rules, and one draw needn't show every extreme that they name: `plane_targets`: block id of each of a plane's two entries in the core sketch; the two may coincide. `plane_signs`: 1 stands for a plus sign, 0 for a minus sign.
All inputs are finite; a program needn't handle non-finite values.
Results may differ from a plain program's by a relative error of at most 0.0003.
Values sent between devices are 32-bit elements; how exact they have to be, the bound alone decides.
A program may use at most 64 MiB of HBM per device.

v0:
```python
import jax
import jax.numpy as jnp
from jax import lax
from jax.sharding import PartitionSpec as P

BLOCK = 16
BLOCKS = 8
precise = lax.Precision.HIGHEST


def gram_of(ranged):
    return jnp.dot(ranged.T, ranged, precision=precise)


def orthonormal_rows(ranged, gram_matrix):
    lower_factor = jnp.linalg.cholesky(gram_matrix)
    return jax.scipy.linalg.solve_triangular(lower_factor, ranged.T, lower=True).T


def selector(targets, sign_values, row_count):
    row_ids = jnp.arange(row_count, dtype=jnp.int32)
    return jnp.sum(
        jnp.where(targets[None, :, :] == row_ids[:, None, None], sign_values[None, :, :], 0.0),
        axis=2,
    )


def body(
    scalar_field, plane_sketch, second_sketch, third_sketch, mixing, plane_targets, plane_signs
):
    planes = scalar_field.shape[0]
    rank_cols = mixing.shape[2]
    along_second = jnp.einsum("pjl,lk->pjk", scalar_field, third_sketch, precision=precise)
    partial_second = jnp.einsum(
        "pjk,pk->jk", along_second, plane_sketch[:, 0, :], precision=precise
    )
    along_third = jnp.einsum("pjl,jk->plk", scalar_field, second_sketch, precision=precise)
    partial_third = jnp.einsum("plk,pk->lk", along_third, plane_sketch[:, 1, :], precision=precise)

    def finish(sketched, mode_index):
        return jnp.dot(sketched, mixing[mode_index], precision=precise)

    rows_second = finish(lax.psum_scatter(partial_second, "gx", scatter_dimension=0, tiled=True), 0)
    rows_third = finish(
        lax.psum_scatter(partial_third, ("gx", "af"), scatter_dimension=0, tiled=True), 1
    )
    gram_second, gram_third = lax.psum((gram_of(rows_second), gram_of(rows_third)), ("gx", "af"))
    factor_second = orthonormal_rows(rows_second, gram_second)
    factor_third = orthonormal_rows(rows_third, gram_third)
    basis_second = lax.all_gather(factor_second, "gx", axis=0, tiled=True)
    basis_third = lax.all_gather(factor_third, ("gx", "af"), axis=0, tiled=True)
    left_side = jnp.einsum("jr,pjl->prl", basis_second, scalar_field, precision=precise)
    projected = jnp.einsum("prl,ls->prs", left_side, basis_third, precision=precise)
    out_rows = BLOCKS * BLOCK // lax.axis_size("gx")
    plane_ids = jnp.arange(plane_targets.shape[0], dtype=jnp.int32)
    all_targets = plane_targets * BLOCK + (plane_ids % BLOCK)[:, None]
    all_signs = (2 * plane_signs - 1).astype(jnp.float32)
    first_plane = lax.axis_index("gx") * planes
    own_targets = lax.dynamic_slice_in_dim(all_targets, first_plane, planes, 0)
    own_signs = lax.dynamic_slice_in_dim(all_signs, first_plane, planes, 0)
    flattened = projected.reshape(planes, -1)
    select = selector(own_targets, own_signs, lax.axis_size("gx") * out_rows)
    partial_core = lax.psum_scatter(
        jnp.dot(select, flattened, precision=precise).reshape(
            lax.axis_size("gx") * out_rows, rank_cols, rank_cols
        ),
        "gx",
        scatter_dimension=0,
        tiled=True,
    )
    core_sketch = lax.psum_scatter(partial_core, "af", scatter_dimension=1, tiled=True)
    return (factor_second, factor_third, core_sketch)


def solution(mesh):
    in_specs = (P("gx", "af", None), P("gx", None, None), P("af", None), P(), P(), P(), P())
    out_specs = (P(("af", "gx"), None), P(("gx", "af"), None), P("gx", "af", None))
    return jax.shard_map(body, mesh=mesh, in_specs=in_specs, out_specs=out_specs, check_vma=False)
```

profile of v0, /device:TPU:2, one launch (start us, length us, event | category | flops | bytes accessed | tf_op | source)
XLA Modules:
  0.0 1100.5 jit_solution(13940723075682379421)
XLA Ops:
  8.2 1.6 fusion.3
  10.7 2.0 fusion.1
  12.7 1.0 copy.72
  13.8 1.3 dynamic-slice
  17.5 168.7 %all-reduce.9.cloned.1.call-done = f32[128,256]{0,1:T(8,128)} async-done(((f32[128,256]{0,1:T(8,128)}), f32[128,256]{0,1:T(8,128)}) %all-reduce.9.cloned.1.call-update) | async-done | bytes 131088
  186.2 1.4 fusion.9
  187.6 0.9 fusion.31
  188.5 254.2 %all-reduce.11.cloned.1.call-done = f32[512,256]{0,1:T(8,128)} async-done(((f32[512,256]{0,1:T(8,128)}), f32[512,256]{0,1:T(8,128)}) %all-reduce.11.cloned.1.call-update) | async-done | bytes 524304
  442.7 1.4 fusion.7
  444.1 0.9 fusion.32
  445.2 243.7 %all-reduce.15.cloned.1.call-done = (f32[128,128]{0,1:T(8,128)}, f32[128,128]{0,1:T(8,128)}) async-done(((f32[128,128]{0,1:T(8,128)}, f32[128,128]{0,1:T(8,128)}), (f32[128,128]{0,1:T(8,128)}, f32[128,128]{0,1:T(8,128)})) %all-reduce.15.cloned.1.call-update) | async-done | bytes 131088 | tf_op jit(solution)/shard_map/psum | solution.py:47
  688.9 0.9 copy.47
  690.7 11.7 %cholesky.44 = f32[128,128]{1,0:T(8,128)S(1)} custom-call(f32[128,128]{1,0:T(8,128)S(1)} %fusion.23), custom_call_target="Cholesky" | custom-call | tf_op jit(solution)/shard_map/jit(cholesky)/cholesky | solution.py:16
  703.8 9.8 custom-call.6
  713.7 41.4 %all-gather = f32[64,2,128]{2,1,0:T(2,128)S(1)} all-gather(f32[1,2,128]{2,1,0:T(2,128)S(1)} %bitcast.107), channel_id=1, replica_groups=mesh['gx'=64,'af'=4] {'gx'}, dimensions={0}, use_global_device_ids=true | all-gather | bytes 66560 | tf_op jit(solution)/shard_map/all_gather | solution.py:50
  755.2 0.9 copy.50
  757.0 11.7 %cholesky.55 = f32[128,128]{1,0:T(8,128)S(1)} custom-call(f32[128,128]{1,0:T(8,128)S(1)} %fusion.20), custom_call_target="Cholesky" | custom-call | tf_op jit(solution)/shard_map/jit(cholesky)/cholesky | solution.py:16
  770.0 9.8 custom-call.7
  780.0 101.1 %all-gather.1 = f32[256,2,128]{2,1,0:T(2,128)S(1)} all-gather(f32[1,2,128]{2,1,0:T(2,128)S(1)} %bitcast.109), channel_id=1, replica_groups=mesh['gx'=64,'af'=4] {'gx','af'}, dimensions={0}, use_global_device_ids=true | all-gather | bytes 263168 | tf_op jit(solution)/shard_map/all_gather | solution.py:51
  882.3 6.8 fusion.5
  889.1 8.1 copy.54
  897.3 147.7 %reduce-scatter.4.cloned.1.call-done = f32[2,128,128]{2,1,0:T(8,128)} async-done(((f32[128,128,128]{2,1,0:T(8,128)}), f32[2,128,128]{2,1,0:T(8,128)}) %reduce-scatter.4.cloned.1.call-update) | async-done | bytes 131088 | tf_op jit(solution)/shard_map/reduce_scatter | solution.py:63
  1044.9 1.6 copy.55
  1047.9 44.8 %all-reduce.13.cloned.1.call-done = f32[2,128,128]{2,0,1:T(2,128)} async-done(((f32[2,128,128]{2,0,1:T(2,128)}), f32[2,128,128]{2,0,1:T(2,128)}) %all-reduce.13.cloned.1.call-update) | async-done | bytes 131088
  (44 shorter events, 11.7 us)
Async XLA Ops:
  7.2 1.1 copy-start
  7.2 179.0 %all-reduce.9.cloned.1.call-start = ((), (), s32[]{:S(2)}) async-start(), calls=%async_computation.2 | async-start | bytes 262144
  10.7 432.0 %all-reduce.11.cloned.1.call-start = ((), (), s32[]{:S(2)}) async-start(), calls=%async_computation.3 | async-start | bytes 1048576
  13.7 675.2 %all-reduce.15.cloned.1.call-start = ((), (), s32[]{:S(2)}) async-start(), calls=%async_computation.5 | async-start | bytes 262144 | tf_op jit(solution)/shard_map/psum | solution.py:47
  445.1 599.9 %reduce-scatter.4.cloned.1.call-start = ((), (), s32[]{:S(2)}) async-start(), calls=%async_computation.1 | async-start | bytes 8519680 | tf_op jit(solution)/shard_map/reduce_scatter | solution.py:63
  713.7 183.4 %copy-start.1 = (f32[128,2]{0,1:T(2,128)}, f32[128,2]{0,1:T(2,128)S(1)}, u32[]{:S(2)}) copy-start(f32[128,2]{0,1:T(2,128)S(1)} %fusion.21) | copy-start | bytes 3076
  780.0 117.2 %copy-start.2 = (f32[128,2]{0,1:T(2,128)}, f32[128,2]{0,1:T(2,128)S(1)}, u32[]{:S(2)}) copy-start(f32[128,2]{0,1:T(2,128)S(1)} %fusion.18) | copy-start | bytes 3076
  897.2 149.4 %copy-start.3 = (u32[256]{0:T(256)S(1)}, u32[256]{0:T(256)}, u32[]{:S(2)}) copy-start(u32[256]{0:T(256)} %constant.78) | copy-start | bytes 3076
  897.2 195.4 %all-reduce.13.cloned.1.call-start = ((), (), s32[]{:S(2)}) async-start(), calls=%async_computation.4 | async-start | bytes 262144
Sparse Core Ops, SparseCore 0:
  11.5 174.6 all-reduce.8
  191.6 251.0 all-reduce.10
  448.3 240.5 all-reduce.14
  897.3 147.5 reduce-scatter.3
  1047.2 45.3 all-reduce.12
where the time goes:
time: 1100 us
  waiting for transfers between devices  859 us (78%)
  blocking collectives  143 us (13%)
  other arithmetic  48.9 us (4%)
  local copies, waits for them, and re-layouts  17.9 us (2%)
  matrix products  16.6 us (2%)
  between operations  15.2 us (1%)
    unnamed x8, waiting for transfers between devices  468 us
    psum x1, waiting for transfers between devices, body(): lax.psum((gram_of(rows_second), gram_of(rows_third)), ('gx', 'af'))  244 us
    reduce_scatter x1, waiting for transfers between devices, body(): lax.psum_scatter(jnp.dot(select, flattened, precision=precise).reshape(la...  148 us
    all_gather x1, blocking collectives, body(): basis_third = lax.all_gather(factor_third, ('gx', 'af'), axis=0, tiled=True)  101 us
    all_gather x1, blocking collectives, body(): basis_second = lax.all_gather(factor_second, 'gx', axis=0, tiled=True)  41.4 us
    another operation x6, other arithmetic, orthonormal_rows(): lower_factor = jnp.linalg.cholesky(gram_matrix)  24.8 us
  transfers between devices with their start and end apart: 5, of which 5 were waited for; matrix products, arithmetic and copies ran while one was open for 1% of the time, Pallas kernels for 0%

commit v1 on v0

--- a/solution.py
+++ b/solution.py
@@ -48,7 +48,8 @@
     factor_second = orthonormal_rows(rows_second, gram_second)
     factor_third = orthonormal_rows(rows_third, gram_third)
     basis_second = lax.all_gather(factor_second, "gx", axis=0, tiled=True)
-    basis_third = lax.all_gather(factor_third, ("gx", "af"), axis=0, tiled=True)
+    stack = jnp.stack([factor_third] * lax.axis_size(("gx", "af")))
+    basis_third = jnp.concatenate(lax.all_to_all(stack, ("gx", "af"), 0, 0), axis=0)
     left_side = jnp.einsum("jr,pjl->prl", basis_second, scalar_field, precision=precise)
     projected = jnp.einsum("prl,ls->prs", left_side, basis_third, precision=precise)
     out_rows = BLOCKS * BLOCK // lax.axis_size("gx")

time: 1100 us -> 1010 us (0.918)
  blocking collectives: 143 us -> 44.9 us
    all_gather x1 -> x0, blocking collectives: 101 us -> none  [body(): basis_third = lax.all_gather(factor_third, ('gx', 'af'), axis=0, tiled=True)]
  transfers between devices with their start and end apart: 5 -> 6, of which waited for: 5 -> 5; matrix products, arithmetic and copies ran while one was open for 1% -> 2% of each run, Pallas kernels for 0% -> 0%
where the time goes in v1:
time: 1010 us
  waiting for transfers between devices  861 us (85%)
  other arithmetic  48.9 us (5%)
  blocking collectives  44.9 us (4%)
  local copies, waits for them, and re-layouts  18.7 us (2%)
  matrix products  16.6 us (2%)
  between operations  15.2 us (2%)
    unnamed x8, waiting for transfers between devices  468 us
    psum x1, waiting for transfers between devices, body(): lax.psum((gram_of(rows_second), gram_of(rows_third)), ('gx', 'af'))  244 us
    reduce_scatter x1, waiting for transfers between devices, body(): lax.psum_scatter(jnp.dot(select, flattened, precision=precise).reshape(la...  149 us
    all_gather x1, blocking collectives, body(): basis_second = lax.all_gather(factor_second, 'gx', axis=0, tiled=True)  44.9 us
    another operation x6, other arithmetic, orthonormal_rows(): lower_factor = jnp.linalg.cholesky(gram_matrix)  24.8 us
    another operation x4, other arithmetic, orthonormal_rows(): jax.scipy.linalg.solve_triangular(lower_factor, ranged.T, lower=True)  20.9 us
  transfers between devices with their start and end apart: 6, of which 5 were waited for; matrix products, arithmetic and copies ran while one was open for 2% of the time, Pallas kernels for 0%

profile of v1, /device:TPU:2, one launch (start us, length us, event | category | flops | bytes accessed | tf_op | source)
XLA Modules:
  0.0 1014.0 jit_solution(18358647308889119063)
XLA Ops:
  8.2 1.6 fusion.3
  10.7 2.0 fusion.1
  12.7 1.0 copy.72
  13.8 1.3 dynamic-slice
  17.5 168.7 %all-reduce.9.cloned.1.call-done = f32[128,256]{0,1:T(8,128)} async-done(((f32[128,256]{0,1:T(8,128)}), f32[128,256]{0,1:T(8,128)}) %all-reduce.9.cloned.1.call-update) | async-done | bytes 131088
  186.2 1.4 fusion.9
  187.6 0.9 fusion.30
  188.5 254.2 %all-reduce.11.cloned.1.call-done = f32[512,256]{0,1:T(8,128)} async-done(((f32[512,256]{0,1:T(8,128)}), f32[512,256]{0,1:T(8,128)}) %all-reduce.11.cloned.1.call-update) | async-done | bytes 524304
  442.7 1.4 fusion.7
  444.1 0.9 fusion.31
  445.2 243.8 %all-reduce.15.cloned.1.call-done = (f32[128,128]{0,1:T(8,128)}, f32[128,128]{0,1:T(8,128)}) async-done(((f32[128,128]{0,1:T(8,128)}, f32[128,128]{0,1:T(8,128)}), (f32[128,128]{0,1:T(8,128)}, f32[128,128]{0,1:T(8,128)})) %all-reduce.15.cloned.1.call-update) | async-done | bytes 131088 | tf_op jit(solution)/shard_map/psum | solution.py:47
  688.9 0.9 copy.47
  690.7 11.7 %cholesky.44 = f32[128,128]{1,0:T(8,128)S(1)} custom-call(f32[128,128]{1,0:T(8,128)S(1)} %fusion.22), custom_call_target="Cholesky" | custom-call | tf_op jit(solution)/shard_map/jit(cholesky)/cholesky | solution.py:16
  703.1 0.9 copy.50
  704.9 11.7 %cholesky.55 = f32[128,128]{1,0:T(8,128)S(1)} custom-call(f32[128,128]{1,0:T(8,128)S(1)} %fusion.19), custom_call_target="Cholesky" | custom-call | tf_op jit(solution)/shard_map/jit(cholesky)/cholesky | solution.py:16
  717.9 9.8 custom-call.7
  728.7 8.5 all-to-all-start
  737.9 9.8 custom-call.6
  747.9 44.9 %all-gather = f32[64,2,128]{2,1,0:T(2,128)S(1)} all-gather(f32[1,2,128]{2,1,0:T(2,128)S(1)} %bitcast.106), channel_id=1, replica_groups=mesh['gx'=64,'af'=4] {'gx'}, dimensions={0}, use_global_device_ids=true | all-gather | bytes 66560 | tf_op jit(solution)/shard_map/all_gather | solution.py:50
  794.0 6.8 fusion.5
  800.8 8.1 copy.54
  808.9 149.5 %reduce-scatter.4.cloned.1.call-done = f32[2,128,128]{2,1,0:T(8,128)} async-done(((f32[128,128,128]{2,1,0:T(8,128)}), f32[2,128,128]{2,1,0:T(8,128)}) %reduce-scatter.4.cloned.1.call-update) | async-done | bytes 131088 | tf_op jit(solution)/shard_map/reduce_scatter | solution.py:64
  958.4 1.6 copy.55
  961.3 44.8 %all-reduce.13.cloned.1.call-done = f32[2,128,128]{2,0,1:T(2,128)} async-done(((f32[2,128,128]{2,0,1:T(2,128)}), f32[2,128,128]{2,0,1:T(2,128)}) %all-reduce.13.cloned.1.call-update) | async-done | bytes 131088
  (46 shorter events, 12.5 us)
Async XLA Ops:
  7.2 1.1 copy-start
  7.2 179.0 %all-reduce.9.cloned.1.call-start = ((), (), s32[]{:S(2)}) async-start(), calls=%async_computation.3 | async-start | bytes 262144
  10.7 432.0 %all-reduce.11.cloned.1.call-start = ((), (), s32[]{:S(2)}) async-start(), calls=%async_computation.4 | async-start | bytes 1048576
  13.7 675.2 %all-reduce.15.cloned.1.call-start = ((), (), s32[]{:S(2)}) async-start(), calls=%async_computation.6 | async-start | bytes 262144 | tf_op jit(solution)/shard_map/psum | solution.py:47
  727.9 80.9 %copy-start.1 = (f32[2,128]{1,0:T(2,128)}, f32[2,128]{1,0:T(2,128)S(1)}, u32[]{:S(2)}) copy-start(f32[2,128]{1,0:T(2,128)S(1)} %convolution_bitcast_fusion.4) | copy-start | bytes 3076
  728.7 64.7 %all-to-all-start = ((f32[256,2,128]{2,1,0:T(2,128)}), f32[256,2,128]{2,1,0:T(2,128)S(1)}, u32[]{:S(2)}, u32[]{:S(2)}) async-start(f32[256,2,128]{2,1,0:T(2,128)} %stack.2), calls=%async_computation | async-start | bytes 524288 | tf_op jit(solution)/shard_map/all_to_all | solution.py:52
  737.2 221.2 %reduce-scatter.4.cloned.1.call-start = ((), (), s32[]{:S(2)}) async-start(), calls=%async_computation.2 | async-start | bytes 8519680 | tf_op jit(solution)/shard_map/reduce_scatter | solution.py:64
  747.9 61.0 %copy-start.2 = (f32[128,2]{0,1:T(2,128)}, f32[128,2]{0,1:T(2,128)S(1)}, u32[]{:S(2)}) copy-start(f32[128,2]{0,1:T(2,128)S(1)} %fusion.20) | copy-start | bytes 3076
  808.9 151.2 %copy-start.3 = (u32[256]{0:T(256)S(1)}, u32[256]{0:T(256)}, u32[]{:S(2)}) copy-start(u32[256]{0:T(256)} %constant.78) | copy-start | bytes 3076
  808.9 197.2 %all-reduce.13.cloned.1.call-start = ((), (), s32[]{:S(2)}) async-start(), calls=%async_computation.5 | async-start | bytes 262144
Sparse Core Ops, SparseCore 0:
  11.5 174.6 all-reduce.8
  191.6 251.0 all-reduce.10
  448.3 240.5 all-reduce.14
  809.0 149.3 reduce-scatter.3
  960.7 45.3 all-reduce.12
